TPU v7x, 32 devices: a whole 2x2x4 slice. The times are simulated.
32 devices in a mesh: grp: 2 (over y), tile: 4 (over z), tm: 2 (over x), ch: 2 (over core).
Axes of the slice: x: 2, y: 2, z: 4, core: 2. Of those that a mesh axis runs over, the one named last changes fastest.
Arguments:
- latent: bfloat16 [8, 8, 64, 512], P(('grp', 'tm'), None, 'tile', 'ch'), parts along dimension 0, may hold values from -340 to 340
- norm_gain: float32 [512], P('ch'), may hold values from 0.1 to 1.9
- norm_shift: float32 [512], P('ch'), may hold values from -3 to 3
- kernel: bfloat16 [3, 3, 3, 512, 512], P(None, None, None, ('ch', 'tile', 'tm')), may hold values from -0.0546875 to 0.0546875
- conv_bias: float32 [512], P('ch'), may hold values from -3 to 3
- blend_profile: int32 [4], replicated, may hold values from 0 to 3
Outputs:
- decoded: bfloat16 [8, 8, 64, 512], P(('grp', 'tm'), None, 'tile', 'ch'), parts along dimension 0
There are 2 independent parts, one for each index of `grp`. A program takes and returns all parts, laid end to end along the dimension named above; an argument that names none is the same for every part. Nothing has to cross between parts.
All inputs are finite; a program needn't handle non-finite values.
Results may differ from a plain program's by a relative error of at most 0.0038.
The roundings to bfloat16 on the way count: a program that leaves them out, or rounds other values in their place, can miss the bound.
Values may be sent and summed in bfloat16 or wider, within the bound.
A program may use at most 64 MiB of HBM per device.

v0:
```python
import jax
import jax.numpy as jnp
from jax import lax
from jax.sharding import PartitionSpec as P

GROUPS = 32
RIM = 4


def with_halo(shard, sides, width):
    for axis, dim in sides:
        size, length = (lax.axis_size(axis), shard.shape[dim])
        up = [(i, (i + 1) % size) for i in range(size - 1)]
        down = [(j, i) for i, j in up]
        last = lax.slice_in_dim(shard, length - width, length, axis=dim)
        leading = lax.slice_in_dim(shard, 0, width, axis=dim)
        before = lax.ppermute(last, axis, up)
        after = lax.ppermute(leading, axis, down)
        shard = jnp.concatenate([before, shard, after], axis=dim)
    return shard


def passed_along(block, axis, distance):
    devices = range(lax.axis_size(axis))
    route = [(i - distance, i) for i in devices if i - distance in devices]
    return lax.ppermute(block, axis, route)


def ramp_weight(profile, position, margin):
    fraction = (position.astype(jnp.float32) + 0.5) / (2.0 * margin)
    exponent = 1.0 + profile.astype(jnp.float32)
    near_part = jnp.power(1.0 - fraction, exponent)
    far_part = jnp.power(fraction, exponent)
    return near_part / (near_part + far_part)


def frame_stats(values, colmask, groups):
    frame_count, row_count, col_count, chan_count = values.shape
    grouped = values.reshape(frame_count, row_count, col_count, groups, chan_count // groups)
    weight = colmask.reshape(1, 1, col_count, 1, 1)
    counted = row_count * (chan_count // groups) * jnp.sum(colmask)
    center = jnp.sum(grouped * weight, axis=(1, 2, 4)) / counted
    spread = (grouped - center[:, None, None, :, None]) * weight
    inverse = lax.rsqrt(jnp.sum(spread * spread, axis=(1, 2, 4)) / counted + 1e-06)
    return (center, inverse)


def activate(values, center, inverse, norm_gain, norm_shift, colmask, timemask, groups):
    frame_count, row_count, col_count, chan_count = values.shape
    grouped = values.reshape(frame_count, row_count, col_count, groups, chan_count // groups)
    normed = (grouped - center[:, None, None, :, None]) * inverse[:, None, None, :, None]
    normed = normed.reshape(values.shape) * norm_gain + norm_shift
    masked = jax.nn.silu(normed) * colmask[None, None, :, None] * timemask[:, None, None, None]
    return masked.astype(jnp.bfloat16)


def conv_taps(padded, kernel_part, frame_count, row_count, col_count):
    in_width = kernel_part.shape[3]
    running = None
    for tap_time in range(3):
        for tap_row in range(3):
            for tap_col in range(3):
                window = padded[
                    tap_time : tap_time + frame_count,
                    tap_row : tap_row + row_count,
                    tap_col : tap_col + col_count,
                ]
                contrib = jnp.dot(
                    window.reshape(-1, in_width),
                    kernel_part[tap_time, tap_row, tap_col],
                    preferred_element_type=jnp.float32,
                )
                running = contrib if running is None else running + contrib
    return running


def on_device(latent, norm_gain, norm_shift, kernel, conv_bias, blend_profile):
    frame_count, row_count, core_cols, chan_half = latent.shape
    out_chans = kernel.shape[4]
    groups = GROUPS // lax.axis_size("ch")
    ncols = core_cols + 2 * RIM
    tile_pos = lax.axis_index("tile")
    tile_count = lax.axis_size("tile")
    window_in = with_halo(latent, (("tile", 2),), RIM)
    cached = passed_along(window_in, "tm", 1)
    frames = jnp.concatenate([cached, window_in], axis=0).astype(jnp.float32)
    column = tile_pos * core_cols - RIM + jnp.arange(ncols, dtype=jnp.int32)
    colmask = ((column >= 0) & (column < tile_count * core_cols)).astype(jnp.float32)
    started = (lax.axis_index("tm") > 0).astype(jnp.float32)
    timemask = jnp.concatenate(
        [jnp.ones((2,), jnp.float32) * started, jnp.ones((frame_count,), jnp.float32)]
    )
    center, inverse = frame_stats(frames, colmask, groups)
    activated = activate(frames, center, inverse, norm_gain, norm_shift, colmask, timemask, groups)
    inputs = (jnp.pad(activated, ((0, 0), (1, 1), (1, 1), (0, 0))),)
    widths = (ncols,)

    def accumulate(shard_rows):
        return tuple(
            (
                conv_taps(source, shard_rows, frame_count, row_count, width_cols)
                for source, width_cols in zip(inputs, widths)
            )
        )

    totals = accumulate(lax.all_gather(kernel, ("tile", "tm"), axis=3, tiled=True))
    shaped = [
        running.reshape(frame_count, row_count, width_cols, out_chans)
        for running, width_cols in zip(totals, widths)
    ]
    joined = shaped[0]
    summed = lax.psum_scatter(joined, "ch", scatter_dimension=3, tiled=True)
    tile_out = (summed + conv_bias).astype(jnp.bfloat16)
    extended = with_halo(tile_out, (("tile", 2),), RIM)
    own_out = tile_out[:, :, RIM : RIM + core_cols]
    left_nbr = extended[:, :, :RIM]
    right_nbr = extended[:, :, ncols + RIM :]
    own_profile = lax.dynamic_index_in_dim(blend_profile, tile_pos, 0, keepdims=False)
    prev_profile = lax.dynamic_index_in_dim(
        blend_profile, jnp.maximum(tile_pos - 1, 0), 0, keepdims=False
    )
    offsets = jnp.arange(RIM, dtype=jnp.int32)
    left_weight = jnp.where(tile_pos > 0, ramp_weight(prev_profile, offsets + RIM, RIM), 0.0)
    right_weight = jnp.where(tile_pos < tile_count - 1, ramp_weight(own_profile, offsets, RIM), 1.0)
    left_wide = left_weight[None, None, :, None]
    right_wide = right_weight[None, None, :, None]
    own_float = own_out.astype(jnp.float32)
    head_cols = own_float[:, :, :RIM] * (1.0 - left_wide) + left_nbr.astype(jnp.float32) * left_wide
    tail_cols = own_float[:, :, core_cols - RIM :] * right_wide + right_nbr.astype(jnp.float32) * (
        1.0 - right_wide
    )
    middle = own_float[:, :, RIM : core_cols - RIM]
    return jnp.concatenate([head_cols, middle, tail_cols], axis=2).astype(jnp.bfloat16)


def solution(mesh):
    in_specs = (
        P(("grp", "tm"), None, "tile", "ch"),
        P("ch"),
        P("ch"),
        P(None, None, None, ("ch", "tile", "tm"), None),
        P("ch"),
        P(),
    )
    out_specs = P(("grp", "tm"), None, "tile", "ch")
    return jax.shard_map(
        on_device, mesh=mesh, in_specs=in_specs, out_specs=out_specs, check_vma=False
    )
```

profile of v0, /device:TPU:0, one launch (start us, length us, event | category | flops | bytes accessed | tf_op | source)
XLA Modules:
  0.0 158.9 jit_solution(7346280072205576620)
XLA Ops:
  6.5 0.7 all-gather.2.cloned.1.call-update
  7.3 0.9 fusion.11
  8.2 4.9 %collective-permute-start = (bf16[2,8,4,256]{3,2,1,0:T(4,128)(2,1)S(1)}, bf16[2,8,4,256]{3,2,1,0:T(4,128)(2,1)S(1)}, u32[]{:S(2)}, u32[]{:S(2)}) collective-permute-start(bf16[2,8,4,256]{3,2,1,0:T(4,128)(2,1)S(1)} %get-tuple-element.40), channel_id=1, source_target_pairs={{0,4},{4,8},{8,12},{1,5},{5,9},{9,13},{2,6},{6,10},{10,14},{3,7},{... | collective-permute-start | bytes 98312 | tf_op jit(solution)/shard_map/ppermute | solution.py:17
  13.2 1.3 collective-permute-start.1
  14.5 0.3 collective-permute-done
  14.7 4.2 %collective-permute-done.1 = bf16[2,8,4,256]{3,2,1,0:T(4,128)(2,1)S(1)} collective-permute-done((bf16[2,8,4,256]{3,2,1,0:T(4,128)(2,1)S(1)}, bf16[2,8,4,256]{3,2,1,0:T(4,128)(2,1)S(1)}, u32[]{:S(2)}, u32[]{:S(2)}) %collective-permute-start.1) | collective-permute-done | bytes 32800 | tf_op jit(solution)/shard_map/ppermute | solution.py:18
  19.0 1.0 pad_maximum_fusion.1
  20.0 3.4 %collective-permute-start.2 = (bf16[2,8,24,256]{3,2,1,0:T(8,128)(2,1)S(1)}, bf16[2,8,24,256]{3,2,1,0:T(8,128)(2,1)S(1)}, u32[]{:S(2)}, u32[]{:S(2)}) collective-permute-start(bf16[2,8,24,256]{3,2,1,0:T(8,128)(2,1)S(1)} %pad_maximum_fusion.1), channel_id=1, source_target_pairs={{0,2},{1,3},{4,6},{5,7},{8,10},{9,11},{12,14},{13,15},{16,18},{17,... | collective-permute-start | bytes 589832 | tf_op jit(solution)/shard_map/ppermute | solution.py:26
  23.4 0.6 fusion.9
  24.7 0.5 concatenate.26
  25.2 1.1 concatenate.24
  26.3 5.6 %collective-permute-done.2 = bf16[2,8,24,256]{3,2,1,0:T(8,128)(2,1)S(1)} collective-permute-done((bf16[2,8,24,256]{3,2,1,0:T(8,128)(2,1)S(1)}, bf16[2,8,24,256]{3,2,1,0:T(8,128)(2,1)S(1)}, u32[]{:S(2)}, u32[]{:S(2)}) %collective-permute-start.2) | collective-permute-done | bytes 196640 | tf_op jit(solution)/shard_map/ppermute | solution.py:26
  31.9 1.1 concatenate.23
  32.9 1.2 fusion
  34.2 1.7 %fusion.3 = f32[4,16]{1,0:T(4,128)S(1)} fusion(f32[4,16]{1,0:T(4,128)S(1)} %broadcast_divide_fusion, f32[24]{0:T(128)S(1)} %and_convert_fusion, bf16[2,8,24,16,16]{4,3,2,1,0:T(8,128)(2,1)S(1)} %concatenate.24, bf16[2,8,24,16,16]{4,3,2,1,0:T(8,128)(2,1)S(1)} %concatenate.23), kind=kLoop, calls=%fused_computation.5 | loop fusion | flops 1179584 | bytes 393824 | tf_op jit(solution)/shard_map/reduce_sum | solution.py:44
  36.2 1.1 multiply_convert_fusion
  37.3 1.1 pad_slice_fusion
  38.4 1.3 pad_slice_fusion.1
  39.7 81.3 %all-gather.2.cloned.1.call-done = bf16[3,3,3,256,512]{4,3,2,1,0:T(8,128)(2,1)} async-done(((bf16[3,3,3,32,512]{4,3,2,1,0:T(8,128)(2,1)}), bf16[3,3,3,256,512]{4,3,2,1,0:T(8,128)(2,1)}) %all-gather.2.cloned.1.call-update) | async-done | bytes 7077904 | tf_op jit(solution)/shard_map/all_gather | solution.py:106
  121.1 1.4 fusion.4
  122.5 1.9 %convolution_add_fusion.25 = f32[384,512]{1,0:T(8,128)S(1)} fusion(f32[384,512]{1,0:T(8,128)S(1)} %fusion.4, bf16[384,256]{1,0:T(8,128)(2,1)} %bitcast.161, bf16[3,3,3,256,512]{4,3,2,1,0:T(8,128)(2,1)} %all-gather.2.cloned.1.call-done), kind=kOutput, calls=%fused_computation.56 | convolution fusion | flops 100859904 | bytes 2031616 | tf_op jit(solution)/shard_map/dot_general | solution.py:68
  124.5 1.2 convolution_add_fusion.24
  125.7 1.2 convolution_add_fusion.23
  126.9 0.3 convolution_add_fusion.22
  127.2 0.3 convolution_add_fusion.21
  127.5 0.3 convolution_add_fusion.20
  127.7 0.3 convolution_add_fusion.19
  128.0 0.3 convolution_add_fusion.18
  128.3 0.3 convolution_add_fusion.17
  128.5 0.3 convolution_add_fusion.16
  128.8 0.3 convolution_add_fusion.15
  129.1 0.3 convolution_add_fusion.14
  129.3 0.3 convolution_add_fusion.13
  129.6 0.3 convolution_add_fusion.12
  130.2 0.3 convolution_add_fusion.10
  130.7 0.3 convolution_add_fusion.8
  131.3 0.3 convolution_add_fusion.6
  131.8 0.3 convolution_add_fusion.4
  132.1 0.3 convolution_add_fusion.3
  132.6 0.3 convolution_add_fusion.1
  132.9 1.1 convolution_add_fusion
  134.1 0.7 fusion.12
  136.1 4.6 %reduce-scatter.2.cloned.1.call-done = f32[2,8,24,256]{3,2,1,0:T(8,128)} async-done(((f32[2,8,24,512]{3,2,1,0:T(8,128)}), f32[2,8,24,256]{3,2,1,0:T(8,128)}) %reduce-scatter.2.cloned.1.call-update) | async-done | bytes 393232 | tf_op jit(solution)/shard_map/reduce_scatter | solution.py:112
  140.7 1.0 add_convert_fusion
  141.7 3.6 %collective-permute-start.3 = (bf16[2,8,4,256]{3,2,1,0:T(4,128)(2,1)S(1)}, bf16[2,8,4,256]{3,2,1,0:T(4,128)(2,1)S(1)}, u32[]{:S(2)}, u32[]{:S(2)}) collective-permute-start(bf16[2,8,4,256]{3,2,1,0:T(4,128)(2,1)S(1)} %get-tuple-element.38), channel_id=1, source_target_pairs={{0,4},{4,8},{8,12},{1,5},{5,9},{9,13},{2,6},{6,10},{10,14},{3,7},{... | collective-permute-start | bytes 98312 | tf_op jit(solution)/shard_map/ppermute | solution.py:17
  145.4 1.3 collective-permute-start.4
  146.9 4.2 %collective-permute-done.4 = bf16[2,8,4,256]{3,2,1,0:T(4,128)(2,1)S(1)} collective-permute-done((bf16[2,8,4,256]{3,2,1,0:T(4,128)(2,1)S(1)}, bf16[2,8,4,256]{3,2,1,0:T(4,128)(2,1)S(1)}, u32[]{:S(2)}, u32[]{:S(2)}) %collective-permute-start.4) | collective-permute-done | bytes 32800 | tf_op jit(solution)/shard_map/ppermute | solution.py:18
  151.3 0.7 pad_maximum_fusion.2
  (48 shorter events, 2.2 us)
Async XLA Ops:
  6.5 29.7 %copy-start.1 = (bf16[2,8,16,256]{3,2,1,0:T(8,128)(2,1)S(1)}, bf16[2,8,16,256]{3,2,1,0:T(8,128)(2,1)}, u32[]{:S(2)}) copy-start(bf16[2,8,16,256]{3,2,1,0:T(8,128)(2,1)} %param.6) | copy-start | bytes 393220
  6.5 29.7 %copy-start.11 = (f32[256]{0:T(256)S(1)}, f32[256]{0:T(256)}, u32[]{:S(2)}) copy-start(f32[256]{0:T(256)} %param.7) | copy-start | bytes 3076
  6.5 29.7 %copy-start.10 = (f32[256]{0:T(256)S(1)}, f32[256]{0:T(256)}, u32[]{:S(2)}) copy-start(f32[256]{0:T(256)} %param.8) | copy-start | bytes 3076
  6.5 114.5 %all-gather.2.cloned.1.call-start = ((), (), s32[]{:S(2)}) async-start(), calls=%async_computation.1 | async-start | bytes 7962624 | tf_op jit(solution)/shard_map/all_gather | solution.py:106
  7.3 133.4 %reduce-scatter.2.cloned.1.call-start = ((), (), s32[]{:S(2)}) async-start(), calls=%async_computation.2 | async-start | bytes 1179648 | tf_op jit(solution)/shard_map/reduce_scatter | solution.py:112
  8.2 6.5 %collective-permute-start = (bf16[2,8,4,256]{3,2,1,0:T(4,128)(2,1)S(1)}, bf16[2,8,4,256]{3,2,1,0:T(4,128)(2,1)S(1)}, u32[]{:S(2)}, u32[]{:S(2)}) collective-permute-start(bf16[2,8,4,256]{3,2,1,0:T(4,128)(2,1)S(1)} %get-tuple-element.40), channel_id=1, source_target_pairs={{0,4},{4,8},{8,12},{1,5},{5,9},{9,13},{2,6},{6,10},{10,14},{3,7},{... | collective-permute-start | bytes 98312 | tf_op jit(solution)/shard_map/ppermute | solution.py:17
  13.2 5.8 %collective-permute-start.1 = (bf16[2,8,4,256]{3,2,1,0:T(4,128)(2,1)S(1)}, bf16[2,8,4,256]{3,2,1,0:T(4,128)(2,1)S(1)}, u32[]{:S(2)}, u32[]{:S(2)}) collective-permute-start(bf16[2,8,4,256]{3,2,1,0:T(4,128)(2,1)S(1)} %get-tuple-element.41), channel_id=1, source_target_pairs={{4,0},{8,4},{12,8},{5,1},{9,5},{13,9},{6,2},{10,6},{14,10},{7,3},{... | collective-permute-start | bytes 98312 | tf_op jit(solution)/shard_map/ppermute | solution.py:18
  20.0 11.9 %collective-permute-start.2 = (bf16[2,8,24,256]{3,2,1,0:T(8,128)(2,1)S(1)}, bf16[2,8,24,256]{3,2,1,0:T(8,128)(2,1)S(1)}, u32[]{:S(2)}, u32[]{:S(2)}) collective-permute-start(bf16[2,8,24,256]{3,2,1,0:T(8,128)(2,1)S(1)} %pad_maximum_fusion.1), channel_id=1, source_target_pairs={{0,2},{1,3},{4,6},{5,7},{8,10},{9,11},{12,14},{13,15},{16,18},{17,... | collective-permute-start | bytes 589832 | tf_op jit(solution)/shard_map/ppermute | solution.py:26
  121.1 5.8 %copy-start = (bf16[3,3,3,256,512]{4,3,2,1,0:T(8,128)(2,1)S(1)}, bf16[3,3,3,256,512]{4,3,2,1,0:T(8,128)(2,1)}, u32[]{:S(2)}) copy-start(bf16[3,3,3,256,512]{4,3,2,1,0:T(8,128)(2,1)} %all-gather.2.cloned.1.call-done) | copy-start | bytes 21233668
  121.1 5.9 %copy-start.8 = (bf16[2,8,24,256]{3,2,1,0:T(8,128)(2,1)S(1)}, bf16[2,8,24,256]{3,2,1,0:T(8,128)(2,1)}, u32[]{:S(2)}) copy-start(bf16[2,8,24,256]{3,2,1,0:T(8,128)(2,1)} %get-tuple-element.34) | copy-start | bytes 589828
  127.5 1.9 %copy-start.7 = (bf16[2,8,24,256]{3,2,1,0:T(8,128)(2,1)S(1)}, bf16[2,8,24,256]{3,2,1,0:T(8,128)(2,1)}, u32[]{:S(2)}) copy-start(bf16[2,8,24,256]{3,2,1,0:T(8,128)(2,1)} %get-tuple-element.33) | copy-start | bytes 589828
  129.6 1.9 %copy-start.6 = (bf16[2,8,24,256]{3,2,1,0:T(8,128)(2,1)S(1)}, bf16[2,8,24,256]{3,2,1,0:T(8,128)(2,1)}, u32[]{:S(2)}) copy-start(bf16[2,8,24,256]{3,2,1,0:T(8,128)(2,1)} %get-tuple-element.29) | copy-start | bytes 589828
  129.9 1.9 %copy-start.5 = (bf16[2,8,24,256]{3,2,1,0:T(8,128)(2,1)S(1)}, bf16[2,8,24,256]{3,2,1,0:T(8,128)(2,1)}, u32[]{:S(2)}) copy-start(bf16[2,8,24,256]{3,2,1,0:T(8,128)(2,1)} %get-tuple-element.32) | copy-start | bytes 589828
  130.1 1.9 %copy-start.4 = (bf16[2,8,24,256]{3,2,1,0:T(8,128)(2,1)S(1)}, bf16[2,8,24,256]{3,2,1,0:T(8,128)(2,1)}, u32[]{:S(2)}) copy-start(bf16[2,8,24,256]{3,2,1,0:T(8,128)(2,1)} %get-tuple-element.30) | copy-start | bytes 589828
  130.4 1.9 %copy-start.3 = (bf16[2,8,24,256]{3,2,1,0:T(8,128)(2,1)S(1)}, bf16[2,8,24,256]{3,2,1,0:T(8,128)(2,1)}, u32[]{:S(2)}) copy-start(bf16[2,8,24,256]{3,2,1,0:T(8,128)(2,1)} %get-tuple-element.31) | copy-start | bytes 589828
  130.7 1.9 %copy-start.2 = (bf16[2,8,24,256]{3,2,1,0:T(8,128)(2,1)S(1)}, bf16[2,8,24,256]{3,2,1,0:T(8,128)(2,1)}, u32[]{:S(2)}) copy-start(bf16[2,8,24,256]{3,2,1,0:T(8,128)(2,1)} %get-tuple-element.28) | copy-start | bytes 589828
  131.2 2.8 %copy-start.9 = (s32[4]{0:T(128)S(1)}, s32[4]{0:T(128)}, u32[]{:S(2)}) copy-start(s32[4]{0:T(128)} %param.11) | copy-start | bytes 52
  131.2 9.4 %copy-start.12 = (f32[256]{0:T(256)S(1)}, f32[256]{0:T(256)}, u32[]{:S(2)}) copy-start(f32[256]{0:T(256)} %param.10) | copy-start | bytes 3076
  141.7 5.2 %collective-permute-start.3 = (bf16[2,8,4,256]{3,2,1,0:T(4,128)(2,1)S(1)}, bf16[2,8,4,256]{3,2,1,0:T(4,128)(2,1)S(1)}, u32[]{:S(2)}, u32[]{:S(2)}) collective-permute-start(bf16[2,8,4,256]{3,2,1,0:T(4,128)(2,1)S(1)} %get-tuple-element.38), channel_id=1, source_target_pairs={{0,4},{4,8},{8,12},{1,5},{5,9},{9,13},{2,6},{6,10},{10,14},{3,7},{... | collective-permute-start | bytes 98312 | tf_op jit(solution)/shard_map/ppermute | solution.py:17
  145.4 5.8 %collective-permute-start.4 = (bf16[2,8,4,256]{3,2,1,0:T(4,128)(2,1)S(1)}, bf16[2,8,4,256]{3,2,1,0:T(4,128)(2,1)S(1)}, u32[]{:S(2)}, u32[]{:S(2)}) collective-permute-start(bf16[2,8,4,256]{3,2,1,0:T(4,128)(2,1)S(1)} %get-tuple-element.39), channel_id=1, source_target_pairs={{4,0},{8,4},{12,8},{5,1},{9,5},{13,9},{6,2},{10,6},{14,10},{7,3},{... | collective-permute-start | bytes 98312 | tf_op jit(solution)/shard_map/ppermute | solution.py:18
Sparse Core Ops, SparseCore 0:
  9.5 111.4 all-gather.1
  134.2 6.4 reduce-scatter.1
where the time goes:
time: 159 us
  waiting for transfers between devices  101 us (64%)
  between operations  15.8 us (10%)
  starting transfers between devices  14.6 us (9%)
  matrix products  12.6 us (8%)
  other arithmetic  7.56 us (5%)
  local copies, waits for them, and re-layouts  7.04 us (4%)
    all_gather x1, waiting for transfers between devices, on_device(): lax.all_gather(kernel, ('tile', 'tm'), axis=3, tiled=True)  81.3 us
    dot_general x27, matrix products, conv_taps(): jnp.dot(window.reshape(-1, in_width), kernel_part[tap_time, tap_row, tap_...  12.6 us
    ppermute x2, starting transfers between devices, with_halo(): before = lax.ppermute(last, axis, up)  8.55 us
    ppermute x2, waiting for transfers between devices, with_halo(): after = lax.ppermute(leading, axis, down)  8.46 us
    ppermute x1, waiting for transfers between devices, passed_along(): return lax.ppermute(block, axis, route)  5.61 us
    reduce_scatter x1, waiting for transfers between devices, on_device(): summed = lax.psum_scatter(joined, 'ch', scatter_dimension=3, tiled=True)  4.61 us
    ppermute x1, starting transfers between devices, passed_along(): return lax.ppermute(block, axis, route)  3.41 us
  transfers between devices with their start and end apart: 7, of which 7 were waited for; matrix products, arithmetic and copies ran while one was open for 8% of the time, Pallas kernels for 0%

commit v1 on v0

--- a/solution.py
+++ b/solution.py
@@ -1,6 +1,9 @@
+import functools
 import jax
 import jax.numpy as jnp
 from jax import lax
+from jax.experimental import pallas as pl
+from jax.experimental.pallas import tpu as pltpu
 from jax.sharding import PartitionSpec as P
 
 GROUPS = 32
@@ -74,7 +77,7 @@
     return running
 
 
-def on_device(latent, norm_gain, norm_shift, kernel, conv_bias, blend_profile):
+def gathered_on_device(latent, norm_gain, norm_shift, kernel, conv_bias, blend_profile):
     frame_count, row_count, core_cols, chan_half = latent.shape
     out_chans = kernel.shape[4]
     groups = GROUPS // lax.axis_size("ch")
@@ -133,6 +136,349 @@
     return jnp.concatenate([head_cols, middle, tail_cols], axis=2).astype(jnp.bfloat16)
 
 
+MESH = pl.DeviceIdType.MESH
+TILES = 4
+BLOCKS = 2
+PARTS = TILES * BLOCKS
+ROWS = 8
+TW = 16
+WIN = TW + 2 * RIM
+IN = 32
+FRAMES = 4
+HALF = 256
+OUT = 512
+F32 = jnp.float32
+BF16 = jnp.bfloat16
+
+
+def iota(shape, dim):
+    return lax.broadcasted_iota(jnp.int32, shape, dim)
+
+
+def exact_dot(a, b):
+    return jnp.dot(a, b, preferred_element_type=F32, precision=lax.Precision.HIGHEST)
+
+
+def fused_kernel(
+    profile, latent, gain, shift, kernel, bias, out,
+    weights, packed, arrived, grid, act, sums, centers, inverses, ramp, lhs, conv,
+    keep, give, took, cross, crossed, send, landed,
+    w_sem, a_send, a_recv, s_send, s_recv, x_send, x_recv, z_send, z_recv,
+):
+    tile = lax.axis_index("tile")
+    tm = lax.axis_index("tm")
+    ch = lax.axis_index("ch")
+    me = tile * BLOCKS + tm
+
+    loads = []
+    for a in range(3):
+        for e in range(3):
+            for side in range(2):
+                start = pl.multiple_of(((ch + side) % 2) * HALF, HALF)
+                loads.append(
+                    pltpu.make_async_copy(
+                        kernel.at[a, :, e, :, pl.ds(start, HALF)],
+                        weights.at[a * 3 + e, pl.ds(0, 3), :, pl.ds(side * HALF, HALF)],
+                        w_sem.at[(a * 3 + e) * 2 + side],
+                    )
+                )
+    for load in loads:
+        load.start()
+
+    barrier = pltpu.get_barrier_semaphore()
+    for d in range(1, PARTS):
+        j = (me + d) % PARTS
+        pl.semaphore_signal(
+            barrier, inc=1, device_id={"tile": j // BLOCKS, "tm": j % BLOCKS}, device_id_type=MESH
+        )
+    pl.semaphore_signal(barrier, inc=1, device_id={"ch": 1 - ch}, device_id_type=MESH)
+
+    row_i, col_i = iota((128, 128), 0), iota((128, 128), 1)
+    turn = jnp.where((row_i % ROWS) * TW + row_i // ROWS == col_i, 1.0, 0.0).astype(BF16)
+    lane_block = iota((64, 128), 1) // IN
+    turned = [
+        jnp.dot(turn, latent[f].reshape(ROWS * TW, HALF), preferred_element_type=F32)
+        for f in range(2)
+    ]
+    for j in range(PARTS):
+        lanes = slice((j // 4) * 128, (j // 4) * 128 + 128)
+        joined = None
+        for k in range(4):
+            piece = turned[k // 2][(k % 2) * 64 : (k % 2) * 64 + 64, lanes]
+            amount = ((k - j % 4) * IN) % 128
+            if amount:
+                piece = pltpu.roll(piece, amount, 1)
+            joined = piece if joined is None else jnp.where(lane_block == k, piece, joined)
+        packed[j] = joined.astype(BF16)
+
+    pl.semaphore_wait(barrier, PARTS)
+    moves = []
+    for d in range(1, PARTS):
+        j = (me + d) % PARTS
+        moves.append(
+            pltpu.make_async_remote_copy(
+                src_ref=packed.at[j],
+                dst_ref=arrived.at[me],
+                send_sem=a_send.at[d - 1],
+                recv_sem=a_recv.at[d - 1],
+                device_id={"tile": j // BLOCKS, "tm": j % BLOCKS},
+                device_id_type=MESH,
+            )
+        )
+    for move in moves:
+        move.start()
+    arrived[me] = packed[me]
+
+    act[:, 0:2] = jnp.zeros((TILES, 2, WIN + 2, ROWS, 128), F32)
+    act[:, 2:, 0:1] = jnp.zeros((TILES, FRAMES, 1, ROWS, 128), F32)
+    act[:, 2:, WIN + 1 :] = jnp.zeros((TILES, FRAMES, 1, ROWS, 128), F32)
+    grid[:, 0:RIM] = jnp.zeros((FRAMES, RIM, ROWS, 128), F32)
+    grid[:, RIM + TILES * TW :] = jnp.zeros((FRAMES, RIM, ROWS, 128), F32)
+    weights[:, 3] = jnp.zeros((9, IN, OUT), BF16)
+    fraction = (iota((8, OUT), 0).astype(F32) + 0.5) / (2.0 * RIM)
+    for margin in range(TILES):
+        p = jnp.full((8, OUT), profile[margin], jnp.int32)
+        near, far = 1.0 - fraction, fraction
+        near_part, far_part = near, far
+        for power in range(1, 4):
+            near_part = jnp.where(p >= power, near_part * near, near_part)
+            far_part = jnp.where(p >= power, far_part * far, far_part)
+        ramp[margin] = near_part / (near_part + far_part)
+    pick = jnp.where(iota((HALF, 128), 0) == me * IN + iota((HALF, 128), 1) % IN, 1.0, 0.0)
+    own_gain = exact_dot(jnp.broadcast_to(gain[...], (8, HALF)), pick)
+    own_shift = exact_dot(jnp.broadcast_to(shift[...], (8, HALF)), pick)
+    group = jnp.where(
+        (row_i // (IN // 2)) == (col_i // (IN // 2)), 1.0, 0.0
+    )
+    spread = [
+        jnp.where((row_i // IN == k) & (row_i % IN == col_i % IN), 1.0, 0.0).astype(BF16)
+        for k in range(4)
+    ]
+
+    for move in moves:
+        move.wait()
+    everything = arrived[...].reshape(PARTS * 64, 128)
+    for k in range(4):
+        wide = jnp.dot(everything, spread[k], preferred_element_type=F32)
+        for s in range(PARTS):
+            first = RIM + (s // BLOCKS) * TW + (k % 2) * (TW // 2)
+            grid[(s % BLOCKS) * 2 + k // 2, first : first + TW // 2] = wide[
+                s * 64 : s * 64 + 64
+            ].reshape(TW // 2, ROWS, 128)
+
+    def present(t):
+        column = t * TW + iota((WIN, ROWS, 128), 0)
+        return jnp.where((column >= RIM) & (column < RIM + TILES * TW), 1.0, 0.0)
+
+    def totals(n, _):
+        t, f = n // FRAMES, n % FRAMES
+        sums[n] = jnp.sum(grid[f, pl.ds(t * TW, WIN)], axis=0)
+        return 0
+
+    pairs = TILES * FRAMES
+    tile_of = iota((pairs, 1, 128), 0) // FRAMES
+    counted = jnp.where((tile_of == 0) | (tile_of == TILES - 1), WIN - RIM, WIN).astype(F32)
+    counted = counted * float(ROWS * (IN // 2))
+    lax.fori_loop(0, pairs, totals, 0)
+
+    def grouped():
+        per_group = exact_dot(sums[...].reshape(pairs * ROWS, 128), group)
+        return jnp.sum(per_group.reshape(pairs, ROWS, 128), axis=1, keepdims=True) / counted
+
+    centers[...] = jnp.broadcast_to(grouped(), (pairs, ROWS, 128))
+
+    def squares(n, _):
+        t, f = n // FRAMES, n % FRAMES
+        apart = (grid[f, pl.ds(t * TW, WIN)] - centers[n]) * present(t)
+        sums[n] = jnp.sum(apart * apart, axis=0)
+        return 0
+
+    lax.fori_loop(0, pairs, squares, 0)
+    inverses[...] = jnp.broadcast_to(lax.rsqrt(grouped() + 1e-06), (pairs, ROWS, 128))
+
+    block_of, row_of = iota((ROWS, 128), 1) // IN, iota((ROWS, 128), 0)
+    inside = (block_of == 1) | ((block_of == 0) & (row_of > 0))
+    inside = jnp.where(inside | ((block_of == 2) & (row_of < ROWS - 1)), 1.0, 0.0)
+
+    def activate_window(n, _):
+        t, f = n // FRAMES, n % FRAMES
+        v = (grid[f, pl.ds(t * TW, WIN)] - centers[n]) * inverses[n] * own_gain + own_shift
+        v = v / (1.0 + jnp.exp(-v)) * present(t)
+        before, after = pltpu.roll(v, 1, 1), pltpu.roll(v, ROWS - 1, 1)
+        v = jnp.where(block_of == 0, before, jnp.where(block_of == 2, after, v))
+        act[t, f + 2, 1 : WIN + 1] = v * inside
+        return 0
+
+    lax.fori_loop(0, pairs, activate_window, 0)
+    for load in loads:
+        load.wait()
+
+    rows_kept = FRAMES * TW * ROWS
+    block_rows = rows_kept // BLOCKS
+
+    def sibling_copy(i):
+        return pltpu.make_async_remote_copy(
+            src_ref=give.at[i], dst_ref=took.at[i],
+            send_sem=s_send.at[i], recv_sem=s_recv.at[i],
+            device_id={"ch": 1 - ch}, device_id_type=MESH,
+        )
+
+    def cross_copy(i):
+        return pltpu.make_async_remote_copy(
+            src_ref=cross.at[i], dst_ref=crossed.at[i],
+            send_sem=x_send.at[i], recv_sem=x_recv.at[i],
+            device_id={"tm": 1 - tm}, device_id_type=MESH,
+        )
+
+    def owner_copy(i):
+        return pltpu.make_async_remote_copy(
+            src_ref=send.at[i], dst_ref=landed.at[i],
+            send_sem=z_send.at[i], recv_sem=z_recv.at[i],
+            device_id={"tile": (tile + 1 + i) % TILES}, device_id_type=MESH,
+        )
+
+    own_rows = pl.ds(pl.multiple_of(tm * block_rows, block_rows), block_rows)
+    other_rows = pl.ds(pl.multiple_of((1 - tm) * block_rows, block_rows), block_rows)
+
+    def convolve(i):
+        t = (tile + 1 + i) % TILES
+        left, right = (t + TILES - 1) % TILES, (t + 1) % TILES
+        for f in range(FRAMES):
+            for a in range(3):
+                for e in range(3):
+                    lanes = slice((a * 3 + e) * 128, (a * 3 + e) * 128 + 128)
+                    row = f * WIN * ROWS
+                    for owner, first, count in (
+                        (t, RIM, TW), (left, TW + RIM, RIM), (right, 0, RIM),
+                    ):
+                        piece = act[owner, f + a, first + e : first + e + count]
+                        lhs[row : row + count * ROWS, lanes] = piece.reshape(
+                            count * ROWS, 128
+                        ).astype(BF16)
+                        row += count * ROWS
+        conv[...] = jnp.dot(
+            lhs[...], weights[...].reshape(9 * 128, OUT), preferred_element_type=F32
+        )
+        has_left = jnp.where(t > 0, 1.0, 0.0)
+        has_right = jnp.where(t < TILES - 1, 1.0, 0.0)
+        for f in range(FRAMES):
+            base = f * WIN * ROWS
+            for c in range(TW):
+                value = conv[base + c * ROWS : base + (c + 1) * ROWS]
+                if c < RIM:
+                    w = ramp[left, RIM + c : RIM + c + 1] * has_left
+                    far = base + (TW + c) * ROWS
+                    value = value * (1.0 - w) + conv[far : far + ROWS] * w
+                if c >= TW - RIM:
+                    j = c - (TW - RIM)
+                    w = 1.0 - (1.0 - ramp[t, j : j + 1]) * has_right
+                    far = base + (TW + RIM + j) * ROWS
+                    value = value * w + conv[far : far + ROWS] * (1.0 - w)
+                row = (f * TW + c) * ROWS
+                keep[i, row : row + ROWS] = value[:, :HALF]
+                give[i, row : row + ROWS] = value[:, HALF:]
+        sibling_copy(i).start()
+
+    def join_sibling(i):
+        sibling_copy(i).wait_recv()
+        cross[i] = (keep[i, other_rows] + took[i, other_rows]).astype(BF16)
+        cross_copy(i).start()
+
+    def join_cross(i):
+        cross_copy(i).wait_recv()
+        return keep[i, own_rows] + took[i, own_rows] + crossed[i].astype(F32)
+
+    def pass_on(i):
+        send[i] = join_cross(i).astype(BF16)
+        owner_copy(i).start()
+
+    def step(s, _):
+        pl.when(s < TILES)(lambda: convolve(s))
+        pl.when((s >= 1) & (s <= TILES))(lambda: join_sibling(s - 1))
+        pl.when((s >= 2) & (s <= TILES))(lambda: pass_on(s - 2))
+        return 0
+
+    lax.fori_loop(0, TILES + 1, step, 0)
+    total = join_cross(TILES - 1)
+    for i in range(TILES - 1):
+        owner_copy(i).wait_recv()
+        total = total + landed[i].astype(F32)
+    result = (total + bias[...]).astype(BF16)
+    back = jnp.where((row_i % TW) * ROWS + row_i // TW == col_i, 1.0, 0.0).astype(BF16)
+    for f in range(2):
+        frame = result[f * TW * ROWS : (f + 1) * TW * ROWS]
+        out[f] = (
+            jnp.dot(back, frame, preferred_element_type=F32)
+            .astype(BF16)
+            .reshape(ROWS, TW, HALF)
+        )
+    for i in range(TILES):
+        sibling_copy(i).wait_send()
+        cross_copy(i).wait_send()
+        if i < TILES - 1:
+            owner_copy(i).wait_send()
+
+
+def fused_on_device(latent, norm_gain, norm_shift, kernel, conv_bias, blend_profile):
+    block_rows = 2 * TW * ROWS
+    dma = pltpu.SemaphoreType.DMA
+    vmem = pl.BlockSpec(memory_space=pltpu.VMEM)
+    return pl.pallas_call(
+        fused_kernel,
+        out_shape=jax.ShapeDtypeStruct((2, ROWS, TW, HALF), BF16),
+        in_specs=[
+            pl.BlockSpec(memory_space=pltpu.SMEM), vmem, vmem, vmem,
+            pl.BlockSpec(memory_space=pl.ANY), vmem,
+        ],
+        out_specs=vmem,
+        scratch_shapes=[
+            pltpu.VMEM((9, 4, IN, OUT), BF16),
+            pltpu.VMEM((PARTS, 64, 128), BF16),
+            pltpu.VMEM((PARTS, 64, 128), BF16),
+            pltpu.VMEM((FRAMES, TILES * TW + 2 * RIM, ROWS, 128), F32),
+            pltpu.VMEM((TILES, FRAMES + 2, WIN + 2, ROWS, 128), F32),
+            pltpu.VMEM((TILES * FRAMES, ROWS, 128), F32),
+            pltpu.VMEM((TILES * FRAMES, ROWS, 128), F32),
+            pltpu.VMEM((TILES * FRAMES, ROWS, 128), F32),
+            pltpu.VMEM((TILES, 2 * RIM, OUT), F32),
+            pltpu.VMEM((FRAMES * WIN * ROWS, 9 * 128), BF16),
+            pltpu.VMEM((FRAMES * WIN * ROWS, OUT), F32),
+            pltpu.VMEM((TILES, 2 * block_rows, HALF), F32),
+            pltpu.VMEM((TILES, 2 * block_rows, HALF), F32),
+            pltpu.VMEM((TILES, 2 * block_rows, HALF), F32),
+            pltpu.VMEM((TILES, block_rows, HALF), BF16),
+            pltpu.VMEM((TILES, block_rows, HALF), BF16),
+            pltpu.VMEM((TILES - 1, block_rows, HALF), BF16),
+            pltpu.VMEM((TILES - 1, block_rows, HALF), BF16),
+            dma((18,)), dma((PARTS - 1,)), dma((PARTS - 1,)),
+            dma((TILES,)), dma((TILES,)), dma((TILES,)), dma((TILES,)),
+            dma((TILES - 1,)), dma((TILES - 1,)),
+        ],
+        compiler_params=pltpu.CompilerParams(
+            collective_id=0, has_side_effects=True, vmem_limit_bytes=48 * 2**20
+        ),
+    )(
+        blend_profile, latent, norm_gain.reshape(1, HALF), norm_shift.reshape(1, HALF),
+        kernel, conv_bias.reshape(1, HALF),
+    )
+
+
+def fits_fused(latent, kernel):
+    sizes = tuple(lax.axis_size(axis) for axis in ("tile", "tm", "ch"))
+    return (
+        sizes == (TILES, BLOCKS, 2)
+        and latent.shape == (2, ROWS, TW, HALF)
+        and kernel.shape == (3, 3, 3, IN, OUT)
+    )
+
+
+def on_device(latent, norm_gain, norm_shift, kernel, conv_bias, blend_profile):
+    arguments = (latent, norm_gain, norm_shift, kernel, conv_bias, blend_profile)
+    if fits_fused(latent, kernel):
+        return fused_on_device(*arguments)
+    return gathered_on_device(*arguments)
+
+
 def solution(mesh):
     in_specs = (
         P(("grp", "tm"), None, "tile", "ch"),

time: 159 us -> 39.1 us (0.25)
  waiting for transfers between devices: 101 us -> 0 us
  Pallas kernels: 0 us -> 35.1 us
  between operations: 15.8 us -> 0.02 us
  starting transfers between devices: 14.6 us -> 0 us
  matrix products: 12.6 us -> 0 us
  other arithmetic: 7.56 us -> 0 us
  local copies, waits for them, and re-layouts: 7.04 us -> 3.44 us
    all_gather x1 -> x0, waiting for transfers between devices: 81.3 us -> none  [on_device(): lax.all_gather(kernel, ('tile', 'tm'), axis=3, tiled=True)]
    pallas_call x0 -> x1, Pallas kernels: none -> 35.1 us  [fused_on_device(): pl.pallas_call(fused_kernel, out_shape=jax.ShapeDtypeStruct((2, ROWS, TW,...]
    ppermute x5 -> x0, waiting for transfers between devices: 14.6 us -> none  [the longest x2 8.46 us: with_halo(): after = lax.ppermute(leading, axis, down)]
    ppermute x5 -> x0, starting transfers between devices: 14.5 us -> none  [the longest x2 8.55 us: with_halo(): before = lax.ppermute(last, axis, up)]
    dot_general x27 -> x0, matrix products: 12.6 us -> none  [conv_taps(): jnp.dot(window.reshape(-1, in_width), kernel_part[tap_time, tap_row, tap_...]
    reduce_scatter x1 -> x0, waiting for transfers between devices: 4.61 us -> none  [on_device(): summed = lax.psum_scatter(joined, 'ch', scatter_dimension=3, tiled=True)]
    reduce_sum x3 -> x0, other arithmetic: 3.51 us -> none  [the longest x1 1.7 us: frame_stats(): jnp.sum(spread * spread, axis=(1, 2, 4)) / counted + 1e-06]
    unnamed x26 -> x13, local copies, waits for them, and re-layouts: 0.06 us -> 3.44 us
  transfers between devices with their start and end apart: 7 -> 0, of which waited for: 7 -> 0; matrix products, arithmetic and copies ran while one was open for 8% -> 0% of each run, Pallas kernels for 0% -> 0%
where the time goes in v1:
time: 39.1 us; the launch traced here: 38.6 us
  Pallas kernels  35.1 us (90%)
  local copies, waits for them, and re-layouts  3.44 us (9%)
    pallas_call x1, Pallas kernels, fused_on_device(): pl.pallas_call(fused_kernel, out_shape=jax.ShapeDtypeStruct((2, ROWS, TW,...  35.1 us
    unnamed x13, local copies, waits for them, and re-layouts  3.44 us

profile of v1, /device:TPU:0, one launch (start us, length us, event | category | flops | bytes accessed | tf_op | source)
XLA Modules:
  0.0 38.6 jit_solution(9447179076776493467)
XLA Ops:
  0.0 0.0 copy-start.3
  0.0 0.0 copy-start.4
  0.0 0.0 copy-start.2
  0.0 0.0 copy-start.5
  0.0 0.7 %copy-done.3 = f32[256]{0:T(256)S(1)} copy-done((f32[256]{0:T(256)S(1)}, f32[256]{0:T(256)}, u32[]{:S(2)}) %copy-start.3) | copy-done | bytes 1048
  0.7 0.0 copy-done.4
  0.7 0.0 copy-done.2
  0.7 0.0 copy-done.5
  0.7 0.0 copy-start
  0.7 1.2 %copy-done = bf16[3,3,3,32,512]{4,3,2,1,0:T(8,128)(2,1)S(1)} copy-done((bf16[3,3,3,32,512]{4,3,2,1,0:T(8,128)(2,1)S(1)}, bf16[3,3,3,32,512]{4,3,2,1,0:T(8,128)(2,1)}, u32[]{:S(2)}) %copy-start) | copy-done | bytes 884760
  1.9 0.0 copy-start.1
  1.9 0.9 %copy-done.1 = bf16[2,8,16,256]{3,2,1,0:T(8,128)(2,1)S(1)} copy-done((bf16[2,8,16,256]{3,2,1,0:T(8,128)(2,1)S(1)}, bf16[2,8,16,256]{3,2,1,0:T(8,128)(2,1)}, u32[]{:S(2)}) %copy-start.1) | copy-done | bytes 131096
  2.8 35.1 %shard_map.64 = bf16[2,8,16,256]{3,2,1,0:T(8,128)(2,1)S(1)} custom-call(s32[4]{0:T(128)S(1)} %copy-done.5, bf16[2,8,16,256]{3,2,1,0:T(8,128)(2,1)S(1)} %copy-done.1, f32[1,256]{1,0:T(1,128)S(1)} %bitcast.3, f32[1,256]{1,0:T(1,128)S(1)} %bitcast.4, bf16[3,3,3,32,512]{4,3,2,1,0:T(8,128)(2,1)S(1)} %copy-done, f32[1,256]{1,0:T(1,128)S(1)} %bitcast.5), custom_call_target="tpu_custom_call" | custom-call | tf_op jit(solution)/shard_map/pallas_call | solution.py:426
  37.9 0.7 %copy.8 = bf16[2,8,16,256]{3,2,1,0:T(8,128)(2,1)} copy(bf16[2,8,16,256]{3,2,1,0:T(8,128)(2,1)S(1)} %shard_map.64) | data formatting | bytes 262144
Async XLA Ops:
  0.0 0.7 %copy-start.3 = (f32[256]{0:T(256)S(1)}, f32[256]{0:T(256)}, u32[]{:S(2)}) copy-start(f32[256]{0:T(256)} %param.8) | copy-start | bytes 3076
  0.0 0.7 %copy-start.4 = (f32[256]{0:T(256)S(1)}, f32[256]{0:T(256)}, u32[]{:S(2)}) copy-start(f32[256]{0:T(256)} %param.10) | copy-start | bytes 3076
  0.0 0.7 %copy-start.2 = (f32[256]{0:T(256)S(1)}, f32[256]{0:T(256)}, u32[]{:S(2)}) copy-start(f32[256]{0:T(256)} %param.7) | copy-start | bytes 3076
  0.0 0.7 %copy-start.5 = (s32[4]{0:T(128)S(1)}, s32[4]{0:T(128)}, u32[]{:S(2)}) copy-start(s32[4]{0:T(128)} %profile.1) | copy-start | bytes 52
  0.7 1.2 %copy-start = (bf16[3,3,3,32,512]{4,3,2,1,0:T(8,128)(2,1)S(1)}, bf16[3,3,3,32,512]{4,3,2,1,0:T(8,128)(2,1)}, u32[]{:S(2)}) copy-start(bf16[3,3,3,32,512]{4,3,2,1,0:T(8,128)(2,1)} %kernel.1) | copy-start | bytes 2654212
  1.9 0.9 %copy-start.1 = (bf16[2,8,16,256]{3,2,1,0:T(8,128)(2,1)S(1)}, bf16[2,8,16,256]{3,2,1,0:T(8,128)(2,1)}, u32[]{:S(2)}) copy-start(bf16[2,8,16,256]{3,2,1,0:T(8,128)(2,1)} %latent.1) | copy-start | bytes 393220

commit v2 on v1

--- a/solution.py
+++ b/solution.py
@@ -160,16 +160,28 @@
 
 
 def fused_kernel(
-    profile, latent, gain, shift, kernel, bias, out,
+    profile_in, latent_in, gain_in, shift_in, kernel, bias_in, out,
+    profile, latent, gain, shift, bias,
     weights, packed, arrived, grid, act, sums, centers, inverses, ramp, lhs, conv,
     keep, give, took, cross, crossed, send, landed,
-    w_sem, a_send, a_recv, s_send, s_recv, x_send, x_recv, z_send, z_recv,
+    i_sem, w_sem, a_send, a_recv, s_send, s_recv, x_send, x_recv, z_send, z_recv,
 ):
     tile = lax.axis_index("tile")
     tm = lax.axis_index("tm")
     ch = lax.axis_index("ch")
     me = tile * BLOCKS + tm
 
+    inputs = [
+        pltpu.make_async_copy(source, target, i_sem.at[n])
+        for n, (source, target) in enumerate(
+            (
+                (latent_in, latent), (profile_in, profile), (gain_in, gain),
+                (shift_in, shift), (bias_in, bias),
+            )
+        )
+    ]
+    for load in inputs:
+        load.start()
     loads = []
     for a in range(3):
         for e in range(3):
@@ -196,6 +208,7 @@
     row_i, col_i = iota((128, 128), 0), iota((128, 128), 1)
     turn = jnp.where((row_i % ROWS) * TW + row_i // ROWS == col_i, 1.0, 0.0).astype(BF16)
     lane_block = iota((64, 128), 1) // IN
+    inputs[0].wait()
     turned = [
         jnp.dot(turn, latent[f].reshape(ROWS * TW, HALF), preferred_element_type=F32)
         for f in range(2)
@@ -235,6 +248,8 @@
     grid[:, 0:RIM] = jnp.zeros((FRAMES, RIM, ROWS, 128), F32)
     grid[:, RIM + TILES * TW :] = jnp.zeros((FRAMES, RIM, ROWS, 128), F32)
     weights[:, 3] = jnp.zeros((9, IN, OUT), BF16)
+    for load in inputs[1:]:
+        load.wait()
     fraction = (iota((8, OUT), 0).astype(F32) + 0.5) / (2.0 * RIM)
     for margin in range(TILES):
         p = jnp.full((8, OUT), profile[margin], jnp.int32)
@@ -316,6 +331,18 @@
     rows_kept = FRAMES * TW * ROWS
     block_rows = rows_kept // BLOCKS
 
+    def target(i):
+        upper = 1 - i // 2
+        lower = ((i + 1) // 2) % 2
+        return 2 * ((tile // 2 + upper) % 2) + (tile % 2 + lower) % 2
+
+    def next_stop(i):
+        later = (i + 1) // 2
+        later = later - later // 2
+        return later * target(i) + (1 - later) * (2 * tile + 1 - 5 * (tile // 2))
+
+    inner = (tile == 1) | (tile == 2)
+
     def sibling_copy(i):
         return pltpu.make_async_remote_copy(
             src_ref=give.at[i], dst_ref=took.at[i],
@@ -334,14 +361,14 @@
         return pltpu.make_async_remote_copy(
             src_ref=send.at[i], dst_ref=landed.at[i],
             send_sem=z_send.at[i], recv_sem=z_recv.at[i],
-            device_id={"tile": (tile + 1 + i) % TILES}, device_id_type=MESH,
+            device_id={"tile": next_stop(i)}, device_id_type=MESH,
         )
 
     own_rows = pl.ds(pl.multiple_of(tm * block_rows, block_rows), block_rows)
     other_rows = pl.ds(pl.multiple_of((1 - tm) * block_rows, block_rows), block_rows)
 
     def convolve(i):
-        t = (tile + 1 + i) % TILES
+        t = target(i)
         left, right = (t + TILES - 1) % TILES, (t + 1) % TILES
         for f in range(FRAMES):
             for a in range(3):
@@ -389,7 +416,14 @@
         return keep[i, own_rows] + took[i, own_rows] + crossed[i].astype(F32)
 
     def pass_on(i):
-        send[i] = join_cross(i).astype(BF16)
+        value = join_cross(i)
+        send[i] = value.astype(BF16)
+
+        @pl.when((i == 1) & inner)
+        def _():
+            owner_copy(0).wait_recv()
+            send[i] = (value + landed[0].astype(F32)).astype(BF16)
+
         owner_copy(i).start()
 
     def step(s, _):
@@ -400,7 +434,13 @@
 
     lax.fori_loop(0, TILES + 1, step, 0)
     total = join_cross(TILES - 1)
-    for i in range(TILES - 1):
+
+    @pl.when(jnp.logical_not(inner))
+    def _():
+        owner_copy(0).wait_recv()
+
+    total = total + jnp.where(inner, 0.0, landed[0].astype(F32))
+    for i in range(1, TILES - 1):
         owner_copy(i).wait_recv()
         total = total + landed[i].astype(F32)
     result = (total + bias[...]).astype(BF16)
@@ -422,16 +462,17 @@
 def fused_on_device(latent, norm_gain, norm_shift, kernel, conv_bias, blend_profile):
     block_rows = 2 * TW * ROWS
     dma = pltpu.SemaphoreType.DMA
-    vmem = pl.BlockSpec(memory_space=pltpu.VMEM)
+    hbm = pl.BlockSpec(memory_space=pltpu.MemorySpace.HBM)
+    vector = pltpu.VMEM((1, HALF), F32)
     return pl.pallas_call(
         fused_kernel,
         out_shape=jax.ShapeDtypeStruct((2, ROWS, TW, HALF), BF16),
-        in_specs=[
-            pl.BlockSpec(memory_space=pltpu.SMEM), vmem, vmem, vmem,
-            pl.BlockSpec(memory_space=pl.ANY), vmem,
-        ],
-        out_specs=vmem,
+        in_specs=[hbm] * 6,
+        out_specs=pl.BlockSpec(memory_space=pltpu.VMEM),
         scratch_shapes=[
+            pltpu.SMEM((TILES,), jnp.int32),
+            pltpu.VMEM((2, ROWS, TW, HALF), BF16),
+            vector, vector, vector,
             pltpu.VMEM((9, 4, IN, OUT), BF16),
             pltpu.VMEM((PARTS, 64, 128), BF16),
             pltpu.VMEM((PARTS, 64, 128), BF16),
@@ -450,12 +491,12 @@
             pltpu.VMEM((TILES, block_rows, HALF), BF16),
             pltpu.VMEM((TILES - 1, block_rows, HALF), BF16),
             pltpu.VMEM((TILES - 1, block_rows, HALF), BF16),
-            dma((18,)), dma((PARTS - 1,)), dma((PARTS - 1,)),
+            dma((5,)), dma((18,)), dma((PARTS - 1,)), dma((PARTS - 1,)),
             dma((TILES,)), dma((TILES,)), dma((TILES,)), dma((TILES,)),
             dma((TILES - 1,)), dma((TILES - 1,)),
         ],
         compiler_params=pltpu.CompilerParams(
-            collective_id=0, has_side_effects=True, vmem_limit_bytes=48 * 2**20
+            collective_id=0, has_side_effects=True, vmem_limit_bytes=63 * 2**20
         ),
     )(
         blend_profile, latent, norm_gain.reshape(1, HALF), norm_shift.reshape(1, HALF),

time: 39.1 us -> 36.7 us (0.939)
  local copies, waits for them, and re-layouts: 3.44 us -> 1.57 us
    unnamed x13 -> x1, local copies, waits for them, and re-layouts: 3.44 us -> 1.57 us
where the time goes in v2:
time: 36.7 us; the launch traced here: 36.6 us
  Pallas kernels  35 us (95%)
  local copies, waits for them, and re-layouts  1.57 us (4%)
    pallas_call x1, Pallas kernels, fused_on_device(): pl.pallas_call(fused_kernel, out_shape=jax.ShapeDtypeStruct((2, ROWS, TW,...  35 us
    unnamed x1, local copies, waits for them, and re-layouts  1.57 us

profile of v2, /device:TPU:0, one launch (start us, length us, event | category | flops | bytes accessed | tf_op | source)
XLA Modules:
  0.0 36.6 jit_solution(18277688069054218963)
XLA Ops:
  0.0 35.0 %shard_map.64 = bf16[2,8,16,256]{3,2,1,0:T(8,128)(2,1)} custom-call(s32[4]{0:T(128)} %profile_in.1, bf16[2,8,16,256]{3,2,1,0:T(8,128)(2,1)} %latent_in.1, f32[1,256]{1,0:T(1,128)} %bitcast.3, f32[1,256]{1,0:T(1,128)} %bitcast.4, bf16[3,3,3,32,512]{4,3,2,1,0:T(8,128)(2,1)} %kernel.1, f32[1,256]{1,0:T(1,128)} %bitcast.5), custom_call_target="tpu_custom_call" | custom-call | tf_op jit(solution)/shard_map/pallas_call | solution.py:467
  35.0 1.6 %copy.8 = bf16[2,8,16,256]{3,2,1,0:T(8,128)(2,1)} copy(bf16[2,8,16,256]{3,2,1,0:T(8,128)(2,1)} %shard_map.64) | data formatting | bytes 262144

commit v3 on v2

--- a/solution.py
+++ b/solution.py
@@ -328,9 +328,6 @@
     for load in loads:
         load.wait()
 
-    rows_kept = FRAMES * TW * ROWS
-    block_rows = rows_kept // BLOCKS
-
     def target(i):
         upper = 1 - i // 2
         lower = ((i + 1) // 2) % 2
@@ -343,10 +340,10 @@
 
     inner = (tile == 1) | (tile == 2)
 
-    def sibling_copy(i):
+    def sibling_copy(i, part):
         return pltpu.make_async_remote_copy(
-            src_ref=give.at[i], dst_ref=took.at[i],
-            send_sem=s_send.at[i], recv_sem=s_recv.at[i],
+            src_ref=give.at[i, part], dst_ref=took.at[i, part],
+            send_sem=s_send.at[i * 2 + part], recv_sem=s_recv.at[i * 2 + part],
             device_id={"ch": 1 - ch}, device_id_type=MESH,
         )
 
@@ -364,13 +361,11 @@
             device_id={"tile": next_stop(i)}, device_id_type=MESH,
         )
 
-    own_rows = pl.ds(pl.multiple_of(tm * block_rows, block_rows), block_rows)
-    other_rows = pl.ds(pl.multiple_of((1 - tm) * block_rows, block_rows), block_rows)
-
-    def convolve(i):
+    def convolve(i, part):
+        start = ((tm + 1 + part) % BLOCKS) * 2
         t = target(i)
         left, right = (t + TILES - 1) % TILES, (t + 1) % TILES
-        for f in range(FRAMES):
+        for f in range(2):
             for a in range(3):
                 for e in range(3):
                     lanes = slice((a * 3 + e) * 128, (a * 3 + e) * 128 + 128)
@@ -378,7 +373,7 @@
                     for owner, first, count in (
                         (t, RIM, TW), (left, TW + RIM, RIM), (right, 0, RIM),
                     ):
-                        piece = act[owner, f + a, first + e : first + e + count]
+                        piece = act[owner, start + f + a, first + e : first + e + count]
                         lhs[row : row + count * ROWS, lanes] = piece.reshape(
                             count * ROWS, 128
                         ).astype(BF16)
@@ -388,7 +383,7 @@
         )
         has_left = jnp.where(t > 0, 1.0, 0.0)
         has_right = jnp.where(t < TILES - 1, 1.0, 0.0)
-        for f in range(FRAMES):
+        for f in range(2):
             base = f * WIN * ROWS
             for c in range(TW):
                 value = conv[base + c * ROWS : base + (c + 1) * ROWS]
@@ -402,18 +397,19 @@
                     far = base + (TW + RIM + j) * ROWS
                     value = value * w + conv[far : far + ROWS] * (1.0 - w)
                 row = (f * TW + c) * ROWS
-                keep[i, row : row + ROWS] = value[:, :HALF]
-                give[i, row : row + ROWS] = value[:, HALF:]
-        sibling_copy(i).start()
+                keep[i, part, row : row + ROWS] = value[:, :HALF]
+                give[i, part, row : row + ROWS] = value[:, HALF:]
+        sibling_copy(i, part).start()
 
     def join_sibling(i):
-        sibling_copy(i).wait_recv()
-        cross[i] = (keep[i, other_rows] + took[i, other_rows]).astype(BF16)
+        sibling_copy(i, 0).wait_recv()
+        cross[i] = (keep[i, 0] + took[i, 0]).astype(BF16)
         cross_copy(i).start()
 
     def join_cross(i):
+        sibling_copy(i, 1).wait_recv()
         cross_copy(i).wait_recv()
-        return keep[i, own_rows] + took[i, own_rows] + crossed[i].astype(F32)
+        return keep[i, 1] + took[i, 1] + crossed[i].astype(F32)
 
     def pass_on(i):
         value = join_cross(i)
@@ -427,12 +423,13 @@
         owner_copy(i).start()
 
     def step(s, _):
-        pl.when(s < TILES)(lambda: convolve(s))
-        pl.when((s >= 1) & (s <= TILES))(lambda: join_sibling(s - 1))
-        pl.when((s >= 2) & (s <= TILES))(lambda: pass_on(s - 2))
+        convolve(s, 0)
+        convolve(s, 1)
+        join_sibling(s)
+        pl.when(s >= 1)(lambda: pass_on(s - 1))
         return 0
 
-    lax.fori_loop(0, TILES + 1, step, 0)
+    lax.fori_loop(0, TILES, step, 0)
     total = join_cross(TILES - 1)
 
     @pl.when(jnp.logical_not(inner))
@@ -453,7 +450,8 @@
             .reshape(ROWS, TW, HALF)
         )
     for i in range(TILES):
-        sibling_copy(i).wait_send()
+        sibling_copy(i, 0).wait_send()
+        sibling_copy(i, 1).wait_send()
         cross_copy(i).wait_send()
         if i < TILES - 1:
             owner_copy(i).wait_send()
@@ -482,17 +480,17 @@
             pltpu.VMEM((TILES * FRAMES, ROWS, 128), F32),
             pltpu.VMEM((TILES * FRAMES, ROWS, 128), F32),
             pltpu.VMEM((TILES, 2 * RIM, OUT), F32),
-            pltpu.VMEM((FRAMES * WIN * ROWS, 9 * 128), BF16),
-            pltpu.VMEM((FRAMES * WIN * ROWS, OUT), F32),
-            pltpu.VMEM((TILES, 2 * block_rows, HALF), F32),
-            pltpu.VMEM((TILES, 2 * block_rows, HALF), F32),
-            pltpu.VMEM((TILES, 2 * block_rows, HALF), F32),
+            pltpu.VMEM((2 * WIN * ROWS, 9 * 128), BF16),
+            pltpu.VMEM((2 * WIN * ROWS, OUT), F32),
+            pltpu.VMEM((TILES, 2, block_rows, HALF), F32),
+            pltpu.VMEM((TILES, 2, block_rows, HALF), F32),
+            pltpu.VMEM((TILES, 2, block_rows, HALF), F32),
             pltpu.VMEM((TILES, block_rows, HALF), BF16),
             pltpu.VMEM((TILES, block_rows, HALF), BF16),
             pltpu.VMEM((TILES - 1, block_rows, HALF), BF16),
             pltpu.VMEM((TILES - 1, block_rows, HALF), BF16),
             dma((5,)), dma((18,)), dma((PARTS - 1,)), dma((PARTS - 1,)),
-            dma((TILES,)), dma((TILES,)), dma((TILES,)), dma((TILES,)),
+            dma((2 * TILES,)), dma((2 * TILES,)), dma((TILES,)), dma((TILES,)),
             dma((TILES - 1,)), dma((TILES - 1,)),
         ],
         compiler_params=pltpu.CompilerParams(

time: 36.7 us -> 36 us (0.981)
  Pallas kernels: 35 us -> 34.2 us
    pallas_call x1, Pallas kernels: 35 us -> 34.2 us  [fused_on_device(): pl.pallas_call(fused_kernel, out_shape=jax.ShapeDtypeStruct((2, ROWS, TW,...]
where the time goes in v3:
time: 36 us; the launch traced here: 35.8 us
  Pallas kernels  34.2 us (95%)
  local copies, waits for them, and re-layouts  1.57 us (4%)
    pallas_call x1, Pallas kernels, fused_on_device(): pl.pallas_call(fused_kernel, out_shape=jax.ShapeDtypeStruct((2, ROWS, TW,...  34.2 us
    unnamed x1, local copies, waits for them, and re-layouts  1.57 us

profile of v3, /device:TPU:0, one launch (start us, length us, event | category | flops | bytes accessed | tf_op | source)
XLA Modules:
  0.0 35.8 jit_solution(2382943331964318248)
XLA Ops:
  0.0 34.2 %shard_map.64 = bf16[2,8,16,256]{3,2,1,0:T(8,128)(2,1)} custom-call(s32[4]{0:T(128)} %profile_in.1, bf16[2,8,16,256]{3,2,1,0:T(8,128)(2,1)} %latent_in.1, f32[1,256]{1,0:T(1,128)} %bitcast.3, f32[1,256]{1,0:T(1,128)} %bitcast.4, bf16[3,3,3,32,512]{4,3,2,1,0:T(8,128)(2,1)} %kernel.1, f32[1,256]{1,0:T(1,128)} %bitcast.5), custom_call_target="tpu_custom_call" | custom-call | tf_op jit(solution)/shard_map/pallas_call | solution.py:465
  34.3 1.6 %copy.8 = bf16[2,8,16,256]{3,2,1,0:T(8,128)(2,1)} copy(bf16[2,8,16,256]{3,2,1,0:T(8,128)(2,1)} %shard_map.64) | data formatting | bytes 262144

commit v4 on v3

--- a/solution.py
+++ b/solution.py
@@ -398,18 +398,18 @@
                     value = value * w + conv[far : far + ROWS] * (1.0 - w)
                 row = (f * TW + c) * ROWS
                 keep[i, part, row : row + ROWS] = value[:, :HALF]
-                give[i, part, row : row + ROWS] = value[:, HALF:]
+                give[i, part, row : row + ROWS] = value[:, HALF:].astype(BF16)
         sibling_copy(i, part).start()
 
     def join_sibling(i):
         sibling_copy(i, 0).wait_recv()
-        cross[i] = (keep[i, 0] + took[i, 0]).astype(BF16)
+        cross[i] = (keep[i, 0] + took[i, 0].astype(F32)).astype(BF16)
         cross_copy(i).start()
 
     def join_cross(i):
         sibling_copy(i, 1).wait_recv()
         cross_copy(i).wait_recv()
-        return keep[i, 1] + took[i, 1] + crossed[i].astype(F32)
+        return keep[i, 1] + took[i, 1].astype(F32) + crossed[i].astype(F32)
 
     def pass_on(i):
         value = join_cross(i)
@@ -483,8 +483,8 @@
             pltpu.VMEM((2 * WIN * ROWS, 9 * 128), BF16),
             pltpu.VMEM((2 * WIN * ROWS, OUT), F32),
             pltpu.VMEM((TILES, 2, block_rows, HALF), F32),
-            pltpu.VMEM((TILES, 2, block_rows, HALF), F32),
-            pltpu.VMEM((TILES, 2, block_rows, HALF), F32),
+            pltpu.VMEM((TILES, 2, block_rows, HALF), BF16),
+            pltpu.VMEM((TILES, 2, block_rows, HALF), BF16),
             pltpu.VMEM((TILES, block_rows, HALF), BF16),
             pltpu.VMEM((TILES, block_rows, HALF), BF16),
             pltpu.VMEM((TILES - 1, block_rows, HALF), BF16),

time: 36 us -> 35.8 us (level)
  no operation moved by 1% of the time
where the time goes in v4:
time: 35.8 us; the launch traced here: 35.6 us
  Pallas kernels  34.1 us (95%)
  local copies, waits for them, and re-layouts  1.57 us (4%)
    pallas_call x1, Pallas kernels, fused_on_device(): pl.pallas_call(fused_kernel, out_shape=jax.ShapeDtypeStruct((2, ROWS, TW,...  34.1 us
    unnamed x1, local copies, waits for them, and re-layouts  1.57 us

profile of v4, /device:TPU:0, one launch (start us, length us, event | category | flops | bytes accessed | tf_op | source)
XLA Modules:
  0.0 35.6 jit_solution(8333890462068250999)
XLA Ops:
  0.0 34.1 %shard_map.64 = bf16[2,8,16,256]{3,2,1,0:T(8,128)(2,1)} custom-call(s32[4]{0:T(128)} %profile_in.1, bf16[2,8,16,256]{3,2,1,0:T(8,128)(2,1)} %latent_in.1, f32[1,256]{1,0:T(1,128)} %bitcast.3, f32[1,256]{1,0:T(1,128)} %bitcast.4, bf16[3,3,3,32,512]{4,3,2,1,0:T(8,128)(2,1)} %kernel.1, f32[1,256]{1,0:T(1,128)} %bitcast.5), custom_call_target="tpu_custom_call" | custom-call | tf_op jit(solution)/shard_map/pallas_call | solution.py:465
  34.1 1.6 %copy.8 = bf16[2,8,16,256]{3,2,1,0:T(8,128)(2,1)} copy(bf16[2,8,16,256]{3,2,1,0:T(8,128)(2,1)} %shard_map.64) | data formatting | bytes 262144
